TPU v7x, 32 devices: a whole 2x2x4 slice. The times are simulated.
32 devices in a mesh: band: 4 (over y, x), ga: 8 (over z, core).
Axes of the slice: x: 2, y: 2, z: 4, core: 2. Of those that a mesh axis runs over, the one named last changes fastest.
Arguments:
- psi: float32 [4096, 4096], P('band', 'ga'), may hold values from -6 to 6
- lower: float32 [4096, 4096], P('band', 'ga'), as said below
Outputs:
- orthonormal: float32 [4096, 4096], P('band', 'ga')
- block_intersection: float32 [4096, 1024], P('band')
Inputs may be any that keep to these rules, and one draw needn't show every extreme that they name: lower is lower triangular with its diagonal between 1 and 2.
All inputs are finite; a program needn't handle non-finite values.
Results may differ from a plain program's by a relative error of at most 0.00022.
Values sent between devices are 32-bit elements; how exact they have to be, the bound alone decides.
A program may use at most 64 MiB of HBM per device.

v0:
```python
import jax
import jax.numpy as jnp
from jax import lax
from jax.sharding import PartitionSpec as P

BASE = 128
PIECES = 2


def mm(a, b, precision):
    return jnp.matmul(a, b, precision=precision, preferred_element_type=jnp.float32)


def tri_inverse(tile):
    n = tile.shape[0]
    base = min(BASE, n)
    best = lax.Precision.HIGHEST
    blocks = jnp.stack([tile[i : i + base, i : i + base] for i in range(0, n, base)])
    row = lax.broadcasted_iota(jnp.int32, (base, base), 0)
    col = lax.broadcasted_iota(jnp.int32, (base, base), 1)
    inverse = jnp.where(row == col, 1.0 / jnp.where(row == col, blocks, 1.0), 0.0)
    size = 1
    while size < base:
        off = (row // (2 * size) == col // (2 * size)) & (row // size > col // size)
        below = jnp.where(off, blocks, 0.0)
        inverse = inverse - mm(inverse, mm(below, inverse, best), best)
        size *= 2
    while size < n:
        below = jnp.stack(
            [tile[i + size : i + 2 * size, i : i + size] for i in range(0, n, 2 * size)]
        )
        first, second = (inverse[0::2], inverse[1::2])
        corner = -mm(second, mm(below, first, best), best)
        top = jnp.concatenate([first, jnp.zeros_like(first)], axis=2)
        bottom = jnp.concatenate([corner, second], axis=2)
        inverse = jnp.concatenate([top, bottom], axis=1)
        size *= 2
    return inverse[0]


def local(psi, lower):
    high = lax.Precision.HIGH
    myblock = lax.axis_index("band")
    sections = lax.axis_size("band")
    nrows, width = psi.shape
    full_rows = lax.all_gather(lower, "ga", axis=1, tiled=True)
    own_tile = lax.dynamic_slice_in_dim(full_rows, myblock * nrows, nrows, 1)
    inverse = tri_inverse(own_tile)
    span = width // PIECES
    rest = [psi[:, i * span : (i + 1) * span] for i in range(PIECES)]
    for s in range(sections - 1):
        tile = full_rows[:, s * nrows : (s + 1) * nrows]
        for i in range(PIECES):
            ready = mm(inverse, rest[i], high)
            arrived = lax.ppermute(ready, "band", [(s, s + 1)])
            for t in range(s + 2, sections):
                arrived = arrived + lax.ppermute(ready, "band", [(s, t)])
            rest[i] = rest[i] - mm(tile, arrived, high)
    solved = jnp.concatenate([mm(inverse, rest[i], high) for i in range(PIECES)], axis=1)
    mine = lax.dot_general(
        solved, solved, (((1,), (1,)), ((), ())), precision=high, preferred_element_type=jnp.float32
    )
    intersection = lax.psum(mine, "ga") / (width * lax.axis_size("ga"))
    return (solved, intersection)


def solution(mesh):
    return jax.shard_map(
        local,
        mesh=mesh,
        in_specs=(P("band", "ga"), P("band", "ga")),
        out_specs=(P("band", "ga"), P("band", None)),
        check_vma=False,
    )
```

profile of v0, /device:TPU:0, one launch (start us, length us, event | category | flops | bytes accessed | tf_op | source)
XLA Modules:
  0.0 475.6 jit_solution(3111644999195573974)
XLA Ops:
  8.7 154.8 %all-gather.2.cloned.1.call-done = f32[1024,4096]{1,0:T(8,128)} async-done(((f32[1024,512]{1,0:T(8,128)}), f32[1024,4096]{1,0:T(8,128)}) %all-gather.2.cloned.1.call-update) | async-done | bytes 16777232 | tf_op jit(solution)/shard_map/all_gather | solution.py:46
  163.4 0.8 fusion.112
  164.3 0.8 fusion.111
  165.1 0.8 fusion.110
  165.9 0.8 fusion.109
  166.8 0.8 fusion.108
  167.6 0.8 fusion.107
  168.5 0.8 fusion.106
  169.3 0.8 fusion.105
  179.6 1.0 dynamic-slice_bitcast_fusion.5
  182.0 1.1 dynamic-slice_bitcast_fusion.1
  183.1 1.3 fusion.60
  185.5 3.9 fusion.50
  189.4 1.9 fusion.49
  191.2 2.8 fusion.141
  194.1 3.4 collective-permute-start
  197.5 2.3 collective-permute-start.1
  199.8 2.3 collective-permute-start.2
  202.1 2.8 fusion.139
  204.9 2.2 collective-permute-start.6
  207.1 2.3 collective-permute-start.7
  209.4 11.9 %collective-permute-done = f32[1024,256]{1,0:T(8,128)S(1)} collective-permute-done((f32[1024,256]{1,0:T(8,128)}, f32[1024,256]{1,0:T(8,128)S(1)}, u32[]{:S(2)}, u32[]{:S(2)}) %collective-permute-start) | collective-permute-done | bytes 1048608 | tf_op jit(solution)/shard_map/ppermute | solution.py:55
  221.3 2.7 collective-permute-start.8
  224.8 18.9 %collective-permute-done.2 = f32[1024,256]{1,0:T(8,128)} collective-permute-done((f32[1024,256]{1,0:T(8,128)}, f32[1024,256]{1,0:T(8,128)}, u32[]{:S(2)}, u32[]{:S(2)}) %collective-permute-start.2) | collective-permute-done | bytes 1048608 | tf_op jit(solution)/shard_map/ppermute | solution.py:57
  243.7 6.8 %fusion.16 = f32[1024,256]{0,1:T(8,128)S(1)} fusion(f32[1024,256]{0,1:T(8,128)S(1)} %copy.13, f32[1024,4096]{1,0:T(8,128)} %all-gather.2.cloned.1.call-done, f32[1024,256]{1,0:T(8,128)} %collective-permute-done.2, f32[1024,256]{1,0:T(8,128)} %copy-done.4, f32[1024,256]{1,0:T(8,128)} %collective-permute-done.1), kind=kOutput, calls=%fused_computation.20 | convolution fusion | flops 1611399168 | bytes 9437184 | tf_op jit(solution)/shard_map/dot_general | solution.py:11
  250.6 1.9 fusion.155
  252.5 0.9 collective-permute-start.3
  253.3 0.9 collective-permute-start.4
  254.2 12.0 %collective-permute-done.6 = f32[1024,256]{1,0:T(8,128)} collective-permute-done((f32[1024,256]{1,0:T(8,128)}, f32[1024,256]{1,0:T(8,128)}, u32[]{:S(2)}, u32[]{:S(2)}) %collective-permute-start.6) | collective-permute-done | bytes 1048608 | tf_op jit(solution)/shard_map/ppermute | solution.py:55
  266.9 21.2 %collective-permute-done.8 = f32[1024,256]{1,0:T(8,128)} collective-permute-done((f32[1024,256]{1,0:T(8,128)}, f32[1024,256]{1,0:T(8,128)}, u32[]{:S(2)}, u32[]{:S(2)}) %collective-permute-start.8) | collective-permute-done | bytes 1048608 | tf_op jit(solution)/shard_map/ppermute | solution.py:57
  288.0 6.7 %fusion.22 = f32[1024,256]{0,1:T(8,128)S(1)} fusion(f32[1024,256]{0,1:T(8,128)S(1)} %copy.14, f32[1024,4096]{1,0:T(8,128)} %all-gather.2.cloned.1.call-done, f32[1024,256]{1,0:T(8,128)} %collective-permute-done.8, f32[1024,256]{1,0:T(8,128)} %collective-permute-done.6, f32[1024,256]{1,0:T(8,128)} %collective-permute-done.7), kind=kOutput, calls=%fused_computation.22 | convolution fusion | flops 1611399168 | bytes 9437184 | tf_op jit(solution)/shard_map/dot_general | solution.py:11
  294.7 1.9 fusion.148
  297.3 0.9 collective-permute-start.9
  298.3 3.7 fusion.28
  301.9 1.9 fusion.153
  304.6 3.7 fusion.34
  308.2 1.9 fusion.146
  310.1 0.9 collective-permute-start.11
  311.1 3.7 fusion.40
  314.7 1.9 fusion.151
  316.6 3.7 fusion.46
  320.3 1.9 fusion.144
  322.2 1.0 copy-done
  323.2 5.3 %fusion.143 = f32[1024,1024]{1,0:T(8,128)} fusion(f32[1024,256]{0,1:T(8,128)S(1)} %fusion.144, f32[1024,256]{0,1:T(8,128)S(1)} %fusion.151), kind=kOutput, calls=%fused_computation.196 | convolution fusion | flops 3221749760 | bytes 6291456 | tf_op jit(solution)/shard_map/dot_general | solution.py:60
  328.6 1.4 pad_maximum_fusion
  330.0 1.8 copy.9
  331.8 131.5 %all-reduce.5.cloned.1.call-done = f32[1024,1024]{1,0:T(8,128)} async-done(((f32[1024,1024]{1,0:T(8,128)}), f32[1024,1024]{1,0:T(8,128)}) %all-reduce.5.cloned.1.call-update) | async-done | bytes 4194320 | tf_op jit(solution)/shard_map/psum | solution.py:63
  463.3 5.0 %broadcast_multiply_fusion = f32[1024,1024]{1,0:T(8,128)} fusion(f32[1024,1024]{1,0:T(8,128)} %all-reduce.5.cloned.1.call-done), kind=kLoop, calls=%fused_computation.18 | loop fusion | flops 1048576 | bytes 8388608 | tf_op jit(solution)/shard_map/div | solution.py:63
  (79 shorter events, 16.2 us)
Async XLA Ops:
  7.2 156.3 %all-gather.2.cloned.1.call-start = ((), (), s32[]{:S(2)}) async-start(), calls=%async_computation | async-start | bytes 18874368 | tf_op jit(solution)/shard_map/all_gather | solution.py:46
  7.9 455.4 %all-reduce.5.cloned.1.call-start = ((), (), s32[]{:S(2)}) async-start(), calls=%async_computation.1 | async-start | bytes 8388608 | tf_op jit(solution)/shard_map/psum | solution.py:63
  185.5 16.6 %copy-start.5 = (f32[1,512,512]{2,1,0:T(8,128)}, f32[1,512,512]{2,1,0:T(8,128)S(1)}, u32[]{:S(2)}) copy-start(f32[1,512,512]{2,1,0:T(8,128)S(1)} %get-tuple-element.12) | copy-start | bytes 3145732
  185.5 16.6 %copy-start.7 = (f32[1,512,512]{2,1,0:T(8,128)}, f32[1,512,512]{2,1,0:T(8,128)S(1)}, u32[]{:S(2)}) copy-start(f32[1,512,512]{2,1,0:T(8,128)S(1)} %get-tuple-element.13) | copy-start | bytes 3145732
  185.5 5.7 %copy-start.1 = (f32[1024,512]{1,0:T(8,128)S(1)}, f32[1024,512]{1,0:T(8,128)}, u32[]{:S(2)}) copy-start(f32[1024,512]{1,0:T(8,128)} %param.2) | copy-start | bytes 6291460
  191.2 10.9 %copy-start.2 = (f32[1,512,512]{2,1,0:T(8,128)}, f32[1,512,512]{2,1,0:T(8,128)S(1)}, u32[]{:S(2)}) copy-start(f32[1,512,512]{2,1,0:T(8,128)S(1)} %fusion.49) | copy-start | bytes 3145732
  194.1 27.2 %collective-permute-start = (f32[1024,256]{1,0:T(8,128)}, f32[1024,256]{1,0:T(8,128)S(1)}, u32[]{:S(2)}, u32[]{:S(2)}) collective-permute-start(f32[1024,256]{1,0:T(8,128)} %fusion.141), channel_id=1, source_target_pairs={{0,8},{1,9},{2,10},{3,11},{4,12},{5,13},{6,14},{7,15}} | collective-permute-start | bytes 3145736 | tf_op jit(solution)/shard_map/ppermute | solution.py:55
  197.5 27.3 %collective-permute-start.1 = (f32[1024,256]{1,0:T(8,128)}, f32[1024,256]{1,0:T(8,128)}, u32[]{:S(2)}, u32[]{:S(2)}) collective-permute-start(f32[1024,256]{1,0:T(8,128)} %fusion.141), channel_id=1, source_target_pairs={{0,16},{1,17},{2,18},{3,19},{4,20},{5,21},{6,22},{7,23}} | collective-permute-start | bytes 3145736 | tf_op jit(solution)/shard_map/ppermute | solution.py:57
  199.8 43.9 %collective-permute-start.2 = (f32[1024,256]{1,0:T(8,128)}, f32[1024,256]{1,0:T(8,128)}, u32[]{:S(2)}, u32[]{:S(2)}) collective-permute-start(f32[1024,256]{1,0:T(8,128)} %fusion.141), channel_id=1, source_target_pairs={{0,24},{1,25},{2,26},{3,27},{4,28},{5,29},{6,30},{7,31}} | collective-permute-start | bytes 3145736 | tf_op jit(solution)/shard_map/ppermute | solution.py:57
  204.9 61.3 %collective-permute-start.6 = (f32[1024,256]{1,0:T(8,128)}, f32[1024,256]{1,0:T(8,128)}, u32[]{:S(2)}, u32[]{:S(2)}) collective-permute-start(f32[1024,256]{1,0:T(8,128)} %fusion.139), channel_id=1, source_target_pairs={{0,8},{1,9},{2,10},{3,11},{4,12},{5,13},{6,14},{7,15}} | collective-permute-start | bytes 3145736 | tf_op jit(solution)/shard_map/ppermute | solution.py:55
  207.1 59.7 %collective-permute-start.7 = (f32[1024,256]{1,0:T(8,128)}, f32[1024,256]{1,0:T(8,128)}, u32[]{:S(2)}, u32[]{:S(2)}) collective-permute-start(f32[1024,256]{1,0:T(8,128)} %fusion.139), channel_id=1, source_target_pairs={{0,16},{1,17},{2,18},{3,19},{4,20},{5,21},{6,22},{7,23}} | collective-permute-start | bytes 3145736 | tf_op jit(solution)/shard_map/ppermute | solution.py:57
  221.3 2.8 copy-start.4
  221.3 66.7 %collective-permute-start.8 = (f32[1024,256]{1,0:T(8,128)}, f32[1024,256]{1,0:T(8,128)}, u32[]{:S(2)}, u32[]{:S(2)}) collective-permute-start(f32[1024,256]{1,0:T(8,128)} %fusion.139), channel_id=1, source_target_pairs={{0,24},{1,25},{2,26},{3,27},{4,28},{5,29},{6,30},{7,31}} | collective-permute-start | bytes 3145736 | tf_op jit(solution)/shard_map/ppermute | solution.py:57
  224.8 25.8 %copy-start.3 = (f32[1,512,512]{2,1,0:T(8,128)S(1)}, f32[1,512,512]{2,1,0:T(8,128)}, u32[]{:S(2)}) copy-start(f32[1,512,512]{2,1,0:T(8,128)} %copy-done.2) | copy-start | bytes 3145732
  224.8 25.8 %copy-start.6 = (f32[1,512,512]{2,1,0:T(8,128)S(1)}, f32[1,512,512]{2,1,0:T(8,128)}, u32[]{:S(2)}) copy-start(f32[1,512,512]{2,1,0:T(8,128)} %copy-done.5) | copy-start | bytes 3145732
  224.8 25.8 %copy-start.8 = (f32[1,512,512]{2,1,0:T(8,128)S(1)}, f32[1,512,512]{2,1,0:T(8,128)}, u32[]{:S(2)}) copy-start(f32[1,512,512]{2,1,0:T(8,128)} %copy-done.7) | copy-start | bytes 3145732
  243.7 54.5 %slice-start = ((s8[16777216]{0:T(1024)(128)(4,1)}), s8[4194304]{0:T(1024)(128)(4,1)S(1)}, s32[]{:S(2)}) async-start(s8[16777216]{0:T(1024)(128)(4,1)} %bitcast.116), calls=%async_computation.2 | async-start | bytes 8388608
  250.6 47.7 %slice-start.1 = ((s8[16777216]{0:T(1024)(128)(4,1)}), s8[4194304]{0:T(1024)(128)(4,1)S(1)}, s32[]{:S(2)}) async-start(s8[16777216]{0:T(1024)(128)(4,1)} %bitcast.116), calls=%async_computation.3 | async-start | bytes 8388608
  252.5 45.8 %slice-start.2 = ((s8[16777216]{0:T(1024)(128)(4,1)}), s8[4194304]{0:T(1024)(128)(4,1)S(1)}, s32[]{:S(2)}) async-start(s8[16777216]{0:T(1024)(128)(4,1)} %bitcast.116), calls=%async_computation.4 | async-start | bytes 8388608
  252.5 45.7 %collective-permute-start.3 = (f32[1024,256]{1,0:T(8,128)S(1)}, f32[1024,256]{1,0:T(8,128)S(1)}, u32[]{:S(2)}, u32[]{:S(2)}) collective-permute-start(f32[1024,256]{1,0:T(8,128)S(1)} %fusion.155), channel_id=1, source_target_pairs={{8,16},{9,17},{10,18},{11,19},{12,20},{13,21},{14,22},{15,23}} | collective-permute-start | bytes 3145736 | tf_op jit(solution)/shard_map/ppermute | solution.py:55
  253.3 44.9 %collective-permute-start.4 = (f32[1024,256]{1,0:T(8,128)S(1)}, f32[1024,256]{1,0:T(8,128)S(1)}, u32[]{:S(2)}, u32[]{:S(2)}) collective-permute-start(f32[1024,256]{1,0:T(8,128)S(1)} %fusion.155), channel_id=1, source_target_pairs={{8,24},{9,25},{10,26},{11,27},{12,28},{13,29},{14,30},{15,31}} | collective-permute-start | bytes 3145736 | tf_op jit(solution)/shard_map/ppermute | solution.py:57
  294.7 3.6 slice-start.3
  296.6 8.0 %collective-permute-start.10 = (f32[1024,256]{1,0:T(8,128)S(1)}, f32[1024,256]{1,0:T(8,128)S(1)}, u32[]{:S(2)}, u32[]{:S(2)}) collective-permute-start(f32[1024,256]{1,0:T(8,128)S(1)} %fusion.148), channel_id=1, source_target_pairs={{8,24},{9,25},{10,26},{11,27},{12,28},{13,29},{14,30},{15,31}} | collective-permute-start | bytes 3145736 | tf_op jit(solution)/shard_map/ppermute | solution.py:57
  297.3 7.3 %collective-permute-start.9 = (f32[1024,256]{1,0:T(8,128)S(1)}, f32[1024,256]{1,0:T(8,128)S(1)}, u32[]{:S(2)}, u32[]{:S(2)}) collective-permute-start(f32[1024,256]{1,0:T(8,128)S(1)} %fusion.148), channel_id=1, source_target_pairs={{8,16},{9,17},{10,18},{11,19},{12,20},{13,21},{14,22},{15,23}} | collective-permute-start | bytes 3145736 | tf_op jit(solution)/shard_map/ppermute | solution.py:55
  303.8 7.2 %collective-permute-start.5 = (f32[1024,256]{1,0:T(8,128)S(1)}, f32[1024,256]{1,0:T(8,128)S(1)}, u32[]{:S(2)}, u32[]{:S(2)}) collective-permute-start(f32[1024,256]{1,0:T(8,128)S(1)} %fusion.153), channel_id=1, source_target_pairs={{16,24},{17,25},{18,26},{19,27},{20,28},{21,29},{22,30},{23,31}} | collective-permute-start | bytes 3145736 | tf_op jit(solution)/shard_map/ppermute | solution.py:55
  310.1 6.5 %collective-permute-start.11 = (f32[1024,256]{1,0:T(8,128)S(1)}, f32[1024,256]{1,0:T(8,128)S(1)}, u32[]{:S(2)}, u32[]{:S(2)}) collective-permute-start(f32[1024,256]{1,0:T(8,128)S(1)} %fusion.146), channel_id=1, source_target_pairs={{16,24},{17,25},{18,26},{19,27},{20,28},{21,29},{22,30},{23,31}} | collective-permute-start | bytes 3145736 | tf_op jit(solution)/shard_map/ppermute | solution.py:55
  322.2 1.0 copy-start
Sparse Core Ops, SparseCore 0:
  9.6 153.7 all-gather.1
  328.7 134.5 all-reduce.4
where the time goes:
time: 485 us; the launch traced here: 476 us
  waiting for transfers between devices  352 us (73%)
  matrix products  68.4 us (14%)
  starting transfers between devices  20.3 us (4%)
  between operations  15.2 us (3%)
  local copies, waits for them, and re-layouts  12.7 us (3%)
  other arithmetic  7.41 us (2%)
    all_gather x1, waiting for transfers between devices, local(): full_rows = lax.all_gather(lower, 'ga', axis=1, tiled=True)  155 us
    psum x1, waiting for transfers between devices, local(): intersection = lax.psum(mine, 'ga') / (width * lax.axis_size('ga'))  131 us
    dot_general x34, matrix products, mm(): jnp.matmul(a, b, precision=precision, preferred_element_type=jnp.float32)  63.1 us
    ppermute x6, waiting for transfers between devices, local(): arrived = arrived + lax.ppermute(ready, 'band', [(s, t)])  40.7 us
    ppermute x6, waiting for transfers between devices, local(): arrived = lax.ppermute(ready, 'band', [(s, s + 1)])  23.9 us
    ppermute x6, starting transfers between devices, local(): arrived = arrived + lax.ppermute(ready, 'band', [(s, t)])  11.1 us
  transfers between devices with their start and end apart: 14, of which 7 were waited for; matrix products, arithmetic and copies ran while one was open for 9% of the time, Pallas kernels for 0%

commit v1 on v0

--- a/solution.py
+++ b/solution.py
@@ -60,7 +60,7 @@
     mine = lax.dot_general(
         solved, solved, (((1,), (1,)), ((), ())), precision=high, preferred_element_type=jnp.float32
     )
-    intersection = lax.psum(mine, "ga") / (width * lax.axis_size("ga"))
+    intersection = jnp.sum(lax.all_gather(mine, "ga"), axis=0) / (width * lax.axis_size("ga"))
     return (solved, intersection)
 
 

time: 485 us -> 690 us (1.42)
  waiting for transfers between devices: 352 us -> 541 us
  other arithmetic: 7.41 us -> 22.1 us
    all_gather x0 -> x1, waiting for transfers between devices: none -> 321 us  [local(): lax.all_gather(mine, 'ga')]
    psum x1 -> x0, waiting for transfers between devices: 131 us -> none  [local(): intersection = lax.psum(mine, 'ga') / (width * lax.axis_size('ga'))]
    ppermute x6, waiting for transfers between devices: 40.7 us -> 23.9 us  [local(): arrived = arrived + lax.ppermute(ready, 'band', [(s, t)])]
    ppermute x6, waiting for transfers between devices: 23.9 us -> 40.7 us  [local(): arrived = lax.ppermute(ready, 'band', [(s, s + 1)])]
    reduce_sum x0 -> x1, other arithmetic: none -> 14.7 us  [local(): jnp.sum(lax.all_gather(mine, 'ga'), axis=0) / (width * lax.axis_size('ga'))]
  transfers between devices with their start and end apart: 14 -> 14, of which waited for: 7 -> 6; matrix products, arithmetic and copies ran while one was open for 9% -> 6% of each run, Pallas kernels for 0% -> 0%
where the time goes in v1:
time: 690 us; the launch traced here: 681 us
  waiting for transfers between devices  541 us (78%)
  matrix products  68.5 us (10%)
  other arithmetic  22.1 us (3%)
  starting transfers between devices  21.2 us (3%)
  between operations  15.2 us (2%)
  local copies, waits for them, and re-layouts  12.7 us (2%)
    all_gather x1, waiting for transfers between devices, local(): lax.all_gather(mine, 'ga')  321 us
    all_gather x1, waiting for transfers between devices, local(): full_rows = lax.all_gather(lower, 'ga', axis=1, tiled=True)  155 us
    dot_general x34, matrix products, mm(): jnp.matmul(a, b, precision=precision, preferred_element_type=jnp.float32)  63.2 us
    ppermute x6, waiting for transfers between devices, local(): arrived = lax.ppermute(ready, 'band', [(s, s + 1)])  40.7 us
    ppermute x6, waiting for transfers between devices, local(): arrived = arrived + lax.ppermute(ready, 'band', [(s, t)])  23.9 us
    reduce_sum x1, other arithmetic, local(): jnp.sum(lax.all_gather(mine, 'ga'), axis=0) / (width * lax.axis_size('ga'))  14.7 us
  transfers between devices with their start and end apart: 14, of which 6 were waited for; matrix products, arithmetic and copies ran while one was open for 6% of the time, Pallas kernels for 0%

profile of v1, /device:TPU:0, one launch (start us, length us, event | category | flops | bytes accessed | tf_op | source)
XLA Modules:
  0.0 680.8 jit_solution(1425713834197938260)
XLA Ops:
  8.7 154.8 %all-gather.4.cloned.1.call-done = f32[1024,4096]{1,0:T(8,128)} async-done(((f32[1024,512]{1,0:T(8,128)}), f32[1024,4096]{1,0:T(8,128)}) %all-gather.4.cloned.1.call-update) | async-done | bytes 16777232 | tf_op jit(solution)/shard_map/all_gather | solution.py:46
  164.3 0.8 fusion.111
  165.1 0.8 fusion.110
  165.9 0.8 fusion.109
  166.8 0.8 fusion.108
  167.6 0.8 fusion.107
  168.5 0.8 fusion.106
  169.3 0.8 fusion.105
  179.6 1.0 dynamic-slice_bitcast_fusion.5
  182.0 1.1 dynamic-slice_bitcast_fusion.1
  183.1 1.3 fusion.60
  185.5 3.9 fusion.50
  189.4 1.9 fusion.49
  191.2 2.8 fusion.139
  194.0 4.3 collective-permute-start.8
  198.4 2.3 collective-permute-start.7
  200.6 2.3 collective-permute-start.6
  203.0 2.8 fusion.141
  205.8 2.3 collective-permute-start.2
  208.1 2.3 collective-permute-start.1
  210.3 11.8 %collective-permute-done.8 = f32[1024,256]{1,0:T(8,128)S(1)} collective-permute-done((f32[1024,256]{1,0:T(8,128)}, f32[1024,256]{1,0:T(8,128)S(1)}, u32[]{:S(2)}, u32[]{:S(2)}) %collective-permute-start.8) | collective-permute-done | bytes 1048608 | tf_op jit(solution)/shard_map/ppermute | solution.py:57
  222.2 2.7 collective-permute-start
  225.7 18.9 %collective-permute-done.6 = f32[1024,256]{1,0:T(8,128)} collective-permute-done((f32[1024,256]{1,0:T(8,128)}, f32[1024,256]{1,0:T(8,128)}, u32[]{:S(2)}, u32[]{:S(2)}) %collective-permute-start.6) | collective-permute-done | bytes 1048608 | tf_op jit(solution)/shard_map/ppermute | solution.py:55
  244.6 6.8 fusion.22
  251.5 1.9 fusion.148
  253.4 0.9 collective-permute-start.10
  254.2 0.9 collective-permute-start.9
  255.1 12.0 %collective-permute-done.2 = f32[1024,256]{1,0:T(8,128)} collective-permute-done((f32[1024,256]{1,0:T(8,128)}, f32[1024,256]{1,0:T(8,128)}, u32[]{:S(2)}, u32[]{:S(2)}) %collective-permute-start.2) | collective-permute-done | bytes 1048608 | tf_op jit(solution)/shard_map/ppermute | solution.py:57
  267.1 21.8 %collective-permute-done = f32[1024,256]{1,0:T(8,128)} collective-permute-done((f32[1024,256]{1,0:T(8,128)}, f32[1024,256]{1,0:T(8,128)}, u32[]{:S(2)}, u32[]{:S(2)}) %collective-permute-start) | collective-permute-done | bytes 1048608 | tf_op jit(solution)/shard_map/ppermute | solution.py:55
  288.9 6.7 fusion.16
  295.6 1.9 fusion.155
  298.2 0.9 collective-permute-start.3
  299.2 3.7 fusion.34
  302.9 1.9 fusion.146
  305.5 3.7 fusion.28
  309.2 1.9 fusion.153
  311.1 0.9 collective-permute-start.5
  312.0 3.7 fusion.46
  315.7 1.9 fusion.144
  317.6 3.7 fusion.40
  321.3 1.9 fusion.151
  323.2 1.0 copy-done
  324.2 5.3 fusion.143
  329.5 1.4 pad_maximum_fusion
  330.9 1.8 copy.9
  332.7 321.1 %all-gather.6.cloned.1.call-done = f32[8192,1024]{1,0:T(8,128)} async-done(((f32[1024,1024]{1,0:T(8,128)}), f32[8192,1024]{1,0:T(8,128)}) %all-gather.6.cloned.1.call-update) | async-done | bytes 33554448 | tf_op jit(solution)/shard_map/all_gather | solution.py:63
  653.8 14.7 %reduce_sum.9 = f32[1024,1024]{1,0:T(8,128)} reduce(f32[8,1024,1024]{2,1,0:T(8,128)} %bitcast.119, f32[]{:T(128)} %constant.202.clone.1), dimensions={0}, to_apply=%region_0.1 | reduce | flops 7340032 | bytes 37748740 | tf_op jit(solution)/shard_map/reduce_sum | solution.py:63
  668.5 5.0 broadcast_multiply_fusion
  (80 shorter events, 16.4 us)
Async XLA Ops:
  7.2 156.3 %all-gather.4.cloned.1.call-start = ((), (), s32[]{:S(2)}) async-start(), calls=%async_computation | async-start | bytes 18874368 | tf_op jit(solution)/shard_map/all_gather | solution.py:46
  7.9 645.9 %all-gather.6.cloned.1.call-start = ((), (), s32[]{:S(2)}) async-start(), calls=%async_computation.1 | async-start | bytes 37748736 | tf_op jit(solution)/shard_map/all_gather | solution.py:63
  185.5 17.5 %copy-start.5 = (f32[1,512,512]{2,1,0:T(8,128)}, f32[1,512,512]{2,1,0:T(8,128)S(1)}, u32[]{:S(2)}) copy-start(f32[1,512,512]{2,1,0:T(8,128)S(1)} %get-tuple-element.12) | copy-start | bytes 3145732
  185.5 17.5 %copy-start.7 = (f32[1,512,512]{2,1,0:T(8,128)}, f32[1,512,512]{2,1,0:T(8,128)S(1)}, u32[]{:S(2)}) copy-start(f32[1,512,512]{2,1,0:T(8,128)S(1)} %get-tuple-element.13) | copy-start | bytes 3145732
  185.5 5.8 copy-start.1
  191.2 11.8 %copy-start.2 = (f32[1,512,512]{2,1,0:T(8,128)}, f32[1,512,512]{2,1,0:T(8,128)S(1)}, u32[]{:S(2)}) copy-start(f32[1,512,512]{2,1,0:T(8,128)S(1)} %fusion.49) | copy-start | bytes 3145732
  194.0 28.1 %collective-permute-start.8 = (f32[1024,256]{1,0:T(8,128)}, f32[1024,256]{1,0:T(8,128)S(1)}, u32[]{:S(2)}, u32[]{:S(2)}) collective-permute-start(f32[1024,256]{1,0:T(8,128)} %fusion.139), channel_id=1, source_target_pairs={{0,24},{1,25},{2,26},{3,27},{4,28},{5,29},{6,30},{7,31}} | collective-permute-start | bytes 3145736 | tf_op jit(solution)/shard_map/ppermute | solution.py:57
  198.4 27.3 %collective-permute-start.7 = (f32[1024,256]{1,0:T(8,128)}, f32[1024,256]{1,0:T(8,128)}, u32[]{:S(2)}, u32[]{:S(2)}) collective-permute-start(f32[1024,256]{1,0:T(8,128)} %fusion.139), channel_id=1, source_target_pairs={{0,16},{1,17},{2,18},{3,19},{4,20},{5,21},{6,22},{7,23}} | collective-permute-start | bytes 3145736 | tf_op jit(solution)/shard_map/ppermute | solution.py:57
  200.6 44.0 %collective-permute-start.6 = (f32[1024,256]{1,0:T(8,128)}, f32[1024,256]{1,0:T(8,128)}, u32[]{:S(2)}, u32[]{:S(2)}) collective-permute-start(f32[1024,256]{1,0:T(8,128)} %fusion.139), channel_id=1, source_target_pairs={{0,8},{1,9},{2,10},{3,11},{4,12},{5,13},{6,14},{7,15}} | collective-permute-start | bytes 3145736 | tf_op jit(solution)/shard_map/ppermute | solution.py:55
  205.8 61.4 %collective-permute-start.2 = (f32[1024,256]{1,0:T(8,128)}, f32[1024,256]{1,0:T(8,128)}, u32[]{:S(2)}, u32[]{:S(2)}) collective-permute-start(f32[1024,256]{1,0:T(8,128)} %fusion.141), channel_id=1, source_target_pairs={{0,24},{1,25},{2,26},{3,27},{4,28},{5,29},{6,30},{7,31}} | collective-permute-start | bytes 3145736 | tf_op jit(solution)/shard_map/ppermute | solution.py:57
  208.1 59.1 %collective-permute-start.1 = (f32[1024,256]{1,0:T(8,128)}, f32[1024,256]{1,0:T(8,128)}, u32[]{:S(2)}, u32[]{:S(2)}) collective-permute-start(f32[1024,256]{1,0:T(8,128)} %fusion.141), channel_id=1, source_target_pairs={{0,16},{1,17},{2,18},{3,19},{4,20},{5,21},{6,22},{7,23}} | collective-permute-start | bytes 3145736 | tf_op jit(solution)/shard_map/ppermute | solution.py:57
  222.2 2.8 copy-start.4
  222.2 66.7 %collective-permute-start = (f32[1024,256]{1,0:T(8,128)}, f32[1024,256]{1,0:T(8,128)}, u32[]{:S(2)}, u32[]{:S(2)}) collective-permute-start(f32[1024,256]{1,0:T(8,128)} %fusion.141), channel_id=1, source_target_pairs={{0,8},{1,9},{2,10},{3,11},{4,12},{5,13},{6,14},{7,15}} | collective-permute-start | bytes 3145736 | tf_op jit(solution)/shard_map/ppermute | solution.py:55
  225.7 25.8 %copy-start.3 = (f32[1,512,512]{2,1,0:T(8,128)S(1)}, f32[1,512,512]{2,1,0:T(8,128)}, u32[]{:S(2)}) copy-start(f32[1,512,512]{2,1,0:T(8,128)} %copy-done.2) | copy-start | bytes 3145732
  225.7 25.8 %copy-start.6 = (f32[1,512,512]{2,1,0:T(8,128)S(1)}, f32[1,512,512]{2,1,0:T(8,128)}, u32[]{:S(2)}) copy-start(f32[1,512,512]{2,1,0:T(8,128)} %copy-done.5) | copy-start | bytes 3145732
  225.7 25.8 %copy-start.8 = (f32[1,512,512]{2,1,0:T(8,128)S(1)}, f32[1,512,512]{2,1,0:T(8,128)}, u32[]{:S(2)}) copy-start(f32[1,512,512]{2,1,0:T(8,128)} %copy-done.7) | copy-start | bytes 3145732
  244.6 54.5 %slice-start = ((s8[16777216]{0:T(1024)(128)(4,1)}), s8[4194304]{0:T(1024)(128)(4,1)S(1)}, s32[]{:S(2)}) async-start(s8[16777216]{0:T(1024)(128)(4,1)} %bitcast.117), calls=%async_computation.2 | async-start | bytes 8388608
  251.5 47.7 %slice-start.1 = ((s8[16777216]{0:T(1024)(128)(4,1)}), s8[4194304]{0:T(1024)(128)(4,1)S(1)}, s32[]{:S(2)}) async-start(s8[16777216]{0:T(1024)(128)(4,1)} %bitcast.117), calls=%async_computation.3 | async-start | bytes 8388608
  253.4 45.8 %slice-start.2 = ((s8[16777216]{0:T(1024)(128)(4,1)}), s8[4194304]{0:T(1024)(128)(4,1)S(1)}, s32[]{:S(2)}) async-start(s8[16777216]{0:T(1024)(128)(4,1)} %bitcast.117), calls=%async_computation.4 | async-start | bytes 8388608
  253.4 45.7 %collective-permute-start.10 = (f32[1024,256]{1,0:T(8,128)S(1)}, f32[1024,256]{1,0:T(8,128)S(1)}, u32[]{:S(2)}, u32[]{:S(2)}) collective-permute-start(f32[1024,256]{1,0:T(8,128)S(1)} %fusion.148), channel_id=1, source_target_pairs={{8,24},{9,25},{10,26},{11,27},{12,28},{13,29},{14,30},{15,31}} | collective-permute-start | bytes 3145736 | tf_op jit(solution)/shard_map/ppermute | solution.py:57
  254.2 44.9 %collective-permute-start.9 = (f32[1024,256]{1,0:T(8,128)S(1)}, f32[1024,256]{1,0:T(8,128)S(1)}, u32[]{:S(2)}, u32[]{:S(2)}) collective-permute-start(f32[1024,256]{1,0:T(8,128)S(1)} %fusion.148), channel_id=1, source_target_pairs={{8,16},{9,17},{10,18},{11,19},{12,20},{13,21},{14,22},{15,23}} | collective-permute-start | bytes 3145736 | tf_op jit(solution)/shard_map/ppermute | solution.py:55
  295.6 3.6 slice-start.3
  297.5 8.0 %collective-permute-start.4 = (f32[1024,256]{1,0:T(8,128)S(1)}, f32[1024,256]{1,0:T(8,128)S(1)}, u32[]{:S(2)}, u32[]{:S(2)}) collective-permute-start(f32[1024,256]{1,0:T(8,128)S(1)} %fusion.155), channel_id=1, source_target_pairs={{8,24},{9,25},{10,26},{11,27},{12,28},{13,29},{14,30},{15,31}} | collective-permute-start | bytes 3145736 | tf_op jit(solution)/shard_map/ppermute | solution.py:57
  298.2 7.3 %collective-permute-start.3 = (f32[1024,256]{1,0:T(8,128)S(1)}, f32[1024,256]{1,0:T(8,128)S(1)}, u32[]{:S(2)}, u32[]{:S(2)}) collective-permute-start(f32[1024,256]{1,0:T(8,128)S(1)} %fusion.155), channel_id=1, source_target_pairs={{8,16},{9,17},{10,18},{11,19},{12,20},{13,21},{14,22},{15,23}} | collective-permute-start | bytes 3145736 | tf_op jit(solution)/shard_map/ppermute | solution.py:55
  304.8 7.3 %collective-permute-start.11 = (f32[1024,256]{1,0:T(8,128)S(1)}, f32[1024,256]{1,0:T(8,128)S(1)}, u32[]{:S(2)}, u32[]{:S(2)}) collective-permute-start(f32[1024,256]{1,0:T(8,128)S(1)} %fusion.146), channel_id=1, source_target_pairs={{16,24},{17,25},{18,26},{19,27},{20,28},{21,29},{22,30},{23,31}} | collective-permute-start | bytes 3145736 | tf_op jit(solution)/shard_map/ppermute | solution.py:55
  311.1 6.5 collective-permute-start.5
  323.2 1.0 copy-start
Sparse Core Ops, SparseCore 0:
  9.6 153.7 all-gather.3
  329.6 324.1 all-gather.5
